TPU v7x, 32 devices: a whole 2x2x4 slice. The times are simulated.
32 devices in a mesh: row: 2 (over x), col: 8 (over z, core), freq: 2 (over y).
Axes of the slice: x: 2, y: 2, z: 4, core: 2. Of those that a mesh axis runs over, the one named last changes fastest.
Arguments:
- left_data: float32 [2, 2048, 512], P(None, ('freq', 'row'), 'col'), parts along dimension 1, may hold values from -6 to 6
- right_data: float32 [2, 512, 8192], P(None, 'row', ('freq', 'col')), parts along dimension 2, may hold values from -0.1875 to 0.1875
Outputs:
- multiples: float32 [2, 2048, 4096], P(None, ('freq', 'row'), 'col'), parts along dimension 1
There are 2 independent parts, one for each index of `freq`. A program takes and returns all parts, laid end to end along the dimension named above; each array names one. Nothing has to cross between parts.
All inputs are finite; a program needn't handle non-finite values.
Results may differ from a plain program's by a relative error of at most 0.000071.
Values sent between devices are 32-bit elements; how exact they have to be, the bound alone decides.
A program may use at most 64 MiB of HBM per device.

v0:
```python
import functools

import jax
import jax.numpy as jnp
from jax import lax
from jax.experimental import pallas as pl
from jax.experimental.pallas import tpu as pltpu
from jax.sharding import PartitionSpec as P

MESH = pl.DeviceIdType.MESH
LANES = 128


def split(value):
    high = value.astype(jnp.bfloat16)
    return high, (value - high.astype(jnp.float32)).astype(jnp.bfloat16)


def dot(a, b):
    return jnp.dot(a, b, preferred_element_type=jnp.float32)


def three_dots(left_hi, left_lo, w_hi, w_lo):
    return dot(left_hi, w_hi) + (dot(left_hi, w_lo) + dot(left_lo, w_hi))


def in_turn(kr):
    return kr % LANES == 0


def finish(first, done_ref, own_part, left_hi, left_lo, w_hi, w_lo, out_hbm, tail, sem):
    rows, ready = done_ref.shape[1:]
    early = pltpu.make_async_copy(done_ref, out_hbm.at[:, :, pl.ds(0, ready)], sem.at[0])
    early.start()
    copies = [early]
    half = rows // 2
    j = w_hi.shape[0] - 1
    for i in range(2):
        span = pl.ds(i * half, half)
        total = own_part[span, :] + three_dots(
            left_hi[span, first:], left_lo[span, first:], w_hi[j, first:, :], w_lo[j, first:, :])
        tail[0, span, :] = total[:, :LANES]
        tail[1, span, :] = total[:, LANES:]
        copy = pltpu.make_async_copy(
            tail.at[:, span, :], out_hbm.at[:, span, pl.ds(ready, LANES)], sem.at[1 + i])
        copy.start()
        copies.append(copy)
    for copy in copies:
        copy.wait()


def kernel(
    n_row, n_col, left_hbm, right_hbm, out_ref, own_part, left_hi, left_lo, w_hi, w_lo,
    left_f32, right_f32, own_sem, left_send, left_recv, right_send, right_recv,
):
    _, kb, rows = left_hbm.shape
    _, kr, cols = right_hbm.shape
    depth = kb * n_col
    chunks = cols // LANES
    line = n_col // 2

    x = lax.axis_index("row")
    place = lax.axis_index("col")
    z, core = place // 2, lax.rem(place, 2)
    has_next, has_prev = z + 1 < line, z >= 1

    def at(zz, cc):
        return {"col": zz * 2 + cc}

    def peer(d):
        return lax.rem(x + d, n_row)

    barrier = pltpu.get_barrier_semaphore()
    for d in range(1, n_row):
        pl.semaphore_signal(barrier, inc=1, device_id={"row": peer(d)}, device_id_type=MESH)

    @pl.when(has_next)
    def _():
        pl.semaphore_signal(barrier, inc=1, device_id=at(z + 1, core), device_id_type=MESH)

    @pl.when(has_prev)
    def _():
        pl.semaphore_signal(barrier, inc=1, device_id=at(z - 1, core), device_id_type=MESH)

    pl.semaphore_signal(barrier, inc=1, device_id=at(z, 1 - core), device_id_type=MESH)

    own_right = pltpu.make_async_copy(
        right_hbm, right_f32.at[:, pl.ds(pl.multiple_of(x * kr, 8), kr), :], own_sem.at[0])
    own_right.start()
    own_left = pltpu.make_async_copy(
        left_hbm, left_f32.at[:, pl.ds(pl.multiple_of(place * kb, 8), kb), :], own_sem.at[1])
    own_left.start()

    pl.semaphore_wait(barrier, n_row + has_next.astype(jnp.int32) + has_prev.astype(jnp.int32))

    def right_copy(d, j):
        return pltpu.make_async_remote_copy(
            src_ref=right_hbm.at[:, :, pl.ds(j * LANES, LANES)],
            dst_ref=right_f32.at[:, pl.ds(pl.multiple_of(x * kr, 8), kr), pl.ds(j * LANES, LANES)],
            send_sem=right_send.at[d - 1, j],
            recv_sem=right_recv.at[d - 1, j],
            device_id={"row": peer(d)},
            device_id_type=MESH,
        )

    def left_slot(zz, cc, part):
        return left_f32.at[part, pl.ds(pl.multiple_of((zz * 2 + cc) * kb, 8), kb), :]

    def left_copy(way, zz, cc, part, target, own=False):
        return pltpu.make_async_remote_copy(
            src_ref=left_hbm.at[part] if own else left_slot(zz, cc, part),
            dst_ref=left_slot(zz, cc, part),
            send_sem=left_send.at[way, zz, part],
            recv_sem=left_recv.at[cc, zz, part],
            device_id=target,
            device_id_type=MESH,
        )

    def up(zz, part, own=False):
        return left_copy(0, zz, core, part, at(z + 1, core), own)

    def down(zz, part, own=False):
        return left_copy(1, zz, core, part, at(z - 1, core), own)

    def across(zz, part, own=False):
        return left_copy(2, zz, core, part, at(z, 1 - core), own)

    def arrived(zz, cc, part):
        left_copy(2, zz, cc, part, at(z, 1 - core)).wait_recv()

    for part in range(2):
        @pl.when(has_next)
        def _():
            up(z, part, True).start()

        @pl.when(has_prev)
        def _():
            down(z, part, True).start()

    for j in range(chunks):
        for d in range(1, n_row):
            right_copy(d, j).start()
    for part in range(2):
        across(z, part, True).start()

    def to_weights(d, j):
        owner = peer(d)
        span = pl.ds(pl.multiple_of(owner * kr, 8), kr)
        re = split(right_f32[0, span, j * LANES:(j + 1) * LANES])
        im = split(right_f32[1, span, j * LANES:(j + 1) * LANES])
        if in_turn(kr):
            above, below = pl.ds(2 * d * kr, kr), pl.ds((2 * d + 1) * kr, kr)
        else:
            above, below = span, pl.ds(pl.multiple_of(depth + owner * kr, 8), kr)
        for w, a, b in ((w_hi, re[0], im[0]), (w_lo, re[1], im[1])):
            w[j, above, :LANES] = a
            w[j, above, LANES:] = b
            w[j, below, :LANES] = -b
            w[j, below, LANES:] = a

    def convert(g):
        for part in range(2):
            block = left_f32[part, pl.ds(pl.multiple_of(g * LANES, LANES), LANES), :].T
            high, low = split(block)
            if in_turn(kr):
                owner = g * LANES // kr
                turn = lax.rem(owner - x + n_row, n_row)
                first = (2 * turn + part) * kr + g * LANES - owner * kr
            else:
                first = part * depth + g * LANES
            where = pl.ds(pl.multiple_of(first, LANES), LANES)
            left_hi[:, where] = high
            left_lo[:, where] = low

    def early_part():
        if in_turn(kr):
            n = 2 * kr
            own_part[...] = three_dots(
                left_hi[:, :n], left_lo[:, :n], w_hi[chunks - 1, :n, :], w_lo[chunks - 1, :n, :])
        else:
            own_part[...] = jnp.zeros_like(own_part)

    def partner_arrived(zz):
        for part in range(2):
            arrived(zz, 1 - core, part)

    def settle(zz):
        partner_arrived(zz)
        if 2 * kb == LANES:
            convert(zz)

    def right_arrived(j):
        for d in range(1, n_row):
            right_copy(d, j).wait_recv()
            to_weights(n_row - d, j)

    own_right.wait()
    for j in range(chunks):
        to_weights(0, j)
    own_left.wait()

    for d in range(1, line):
        for part in range(2):
            @pl.when(z - d >= 0)
            def _():
                arrived(z - d, core, part)

                @pl.when(has_next)
                def _():
                    up(z - d, part).start()

                across(z - d, part).start()

            @pl.when(z + d < line)
            def _():
                arrived(z + d, core, part)

                @pl.when(has_prev)
                def _():
                    down(z + d, part).start()

                across(z + d, part).start()

        if d == 1:
            settle(z)
        else:
            @pl.when(z - (d - 1) >= 0)
            def _():
                settle(z - (d - 1))

            @pl.when(z + (d - 1) < line)
            def _():
                settle(z + (d - 1))

        if d - 1 < chunks - 1:
            right_arrived(d - 1)

    if line == 1:
        settle(z)
    else:
        @pl.when(z - (line - 1) >= 0)
        def _():
            settle(z - (line - 1))

        @pl.when(z + (line - 1) < line)
        def _():
            settle(z + (line - 1))

    if 2 * kb != LANES:
        for g in range(depth // LANES):
            convert(g)

    for j in range(chunks - 1):
        if j >= line - 1:
            right_arrived(j)
        total = three_dots(left_hi[...], left_lo[...], w_hi[j], w_lo[j])
        out_ref[0, :, j * LANES:(j + 1) * LANES] = total[:, :LANES]
        out_ref[1, :, j * LANES:(j + 1) * LANES] = total[:, LANES:]
        if j == chunks - 3 or (j == 0 and chunks < 3):
            early_part()
    right_arrived(chunks - 1)

    for j in range(chunks):
        for d in range(1, n_row):
            right_copy(d, j).wait_send()
    for part in range(2):
        for d in range(line):
            own = d == 0

            @pl.when(z - d >= 0)
            def _():
                @pl.when(has_next)
                def _():
                    up(z - d, part, own).wait_send()

                across(z - d, part, own).wait_send()

            @pl.when(z + d < line)
            def _():
                @pl.when(has_prev)
                def _():
                    down(z + d, part, own).wait_send()

                if d > 0:
                    across(z + d, part).wait_send()


def body(n_row, n_col, left_data, right_data):
    left = jnp.swapaxes(left_data, 1, 2)
    _, kb, rows = left.shape
    _, kr, cols = right_data.shape
    depth, chunks, line = kb * n_col, cols // LANES, n_col // 2
    vmem = pl.BlockSpec(memory_space=pltpu.VMEM)
    held = pl.pallas_call(
        functools.partial(kernel, n_row, n_col),
        out_shape=[
            jax.ShapeDtypeStruct((2, rows, cols - LANES), jnp.float32),
            jax.ShapeDtypeStruct((rows, 2 * LANES), jnp.float32),
            jax.ShapeDtypeStruct((rows, 2 * depth), jnp.bfloat16),
            jax.ShapeDtypeStruct((rows, 2 * depth), jnp.bfloat16),
            jax.ShapeDtypeStruct((chunks, 2 * depth, 2 * LANES), jnp.bfloat16),
            jax.ShapeDtypeStruct((chunks, 2 * depth, 2 * LANES), jnp.bfloat16),
        ],
        in_specs=[pl.BlockSpec(memory_space=pltpu.HBM)] * 2,
        out_specs=[vmem] * 6,
        scratch_shapes=[
            pltpu.VMEM((2, depth, rows), jnp.float32),
            pltpu.VMEM((2, depth, cols), jnp.float32),
            pltpu.SemaphoreType.DMA((2,)),
            pltpu.SemaphoreType.DMA((3, line, 2)),
            pltpu.SemaphoreType.DMA((2, line, 2)),
            pltpu.SemaphoreType.DMA((n_row - 1, chunks)),
            pltpu.SemaphoreType.DMA((n_row - 1, chunks)),
        ],
        compiler_params=pltpu.CompilerParams(
            collective_id=0, has_side_effects=True, vmem_limit_bytes=32 * 1024 * 1024),
    )(pltpu.with_memory_space_constraint(left, pltpu.HBM), pltpu.with_memory_space_constraint(right_data, pltpu.HBM))
    return pl.pallas_call(
        functools.partial(finish, 2 * kr if in_turn(kr) else 0),
        out_shape=jax.ShapeDtypeStruct((2, rows, cols), jnp.float32),
        in_specs=[vmem] * 6,
        out_specs=pl.BlockSpec(memory_space=pltpu.HBM),
        scratch_shapes=[pltpu.VMEM((2, rows, LANES), jnp.float32), pltpu.SemaphoreType.DMA((3,))],
        compiler_params=pltpu.CompilerParams(vmem_limit_bytes=16 * 1024 * 1024),
    )(*held)


def solution(mesh):
    placed = (P(None, ("freq", "row"), "col"), P(None, "row", ("freq", "col")))
    return jax.shard_map(
        functools.partial(body, mesh.shape["row"], mesh.shape["col"]),
        mesh=mesh, in_specs=placed, out_specs=P(None, ("freq", "row"), "col"), check_vma=False,
    )
```

profile of v0, /device:TPU:0, one launch (start us, length us, event | category | flops | bytes accessed | tf_op | source)
XLA Modules:
  0.0 30.0 jit_solution(4441440149178608989)
XLA Ops:
  0.0 28.2 %shard_map.28 = (f32[2,512,384]{2,1,0:T(8,128)S(1)}, f32[512,256]{1,0:T(8,128)S(1)}, bf16[512,1024]{1,0:T(8,128)(2,1)S(1)}, bf16[512,1024]{1,0:T(8,128)(2,1)S(1)...) custom-call(f32[2,64,512]{2,1,0:T(8,128)} %bitcast.1, f32[2,256,512]{2,1,0:T(8,128)} %right_hbm.1), custom_call_target="tpu_custom_call" | custom-call | tf_op jit(solution)/shard_map/pallas_call | solution.py:294
  28.2 1.8 %shard_map.29 = f32[2,512,512]{2,1,0:T(8,128)} custom-call(f32[2,512,384]{2,1,0:T(8,128)S(1)} %get-tuple-element.11.done_ref, f32[512,256]{1,0:T(8,128)S(1)} %get-tuple-element.12.own_part, bf16[512,1024]{1,0:T(8,128)(2,1)S(1)} %get-tuple-element.13.left_hi, bf16[512,1024]{1,0:T(8,128)(2,1)S(1)} %get-tuple-element.14.left_lo, ...), custom_call_target="tpu_custom_call" | custom-call | tf_op jit(solution)/shard_map/pallas_call | solution.py:318
where the time goes:
time: 30.2 us; the launch traced here: 30 us
  Pallas kernels  30 us (99%)
    pallas_call x1, Pallas kernels, body(): pl.pallas_call(functools.partial(kernel, n_row, n_col), out_shape=[jax.Sh...  28.2 us
    pallas_call x1, Pallas kernels, body(): pl.pallas_call(functools.partial(finish, 2 * kr if in_turn(kr) else 0), o...  1.84 us

commit v1 on v0

v1 whole, which is shorter than its diff:
```python
import functools

import jax
import jax.numpy as jnp
from jax import lax
from jax.experimental import pallas as pl
from jax.experimental.pallas import tpu as pltpu
from jax.sharding import PartitionSpec as P

MESH = pl.DeviceIdType.MESH
LANES = 128
PAIR = 2 * LANES


def split(value):
    high = value.astype(jnp.bfloat16)
    return high, (value - high.astype(jnp.float32)).astype(jnp.bfloat16)


def dot(a, b):
    return jnp.dot(a, b, preferred_element_type=jnp.float32)


def three_dots(left_hi, left_lo, w_hi, w_lo):
    return dot(left_hi, w_hi) + (dot(left_hi, w_lo) + dot(left_lo, w_hi))


def by_slab(kb, kr, line):
    return 2 * kb == LANES and kr % LANES == 0 and line > 1


def right_pieces(kb, kr, line, chunks):
    pieces = [(j, 0, kr) for j in range(chunks)]
    if by_slab(kb, kr, line):
        pieces[-1:] = [(chunks - 1, r, LANES) for r in range(0, kr, LANES)]
    return pieces


def write(done_ref, out_hbm, sem):
    copy = pltpu.make_async_copy(done_ref, out_hbm, sem.at[0])
    copy.start()
    copy.wait()


def kernel(
    n_row, n_col, left_hbm, right_hbm, out_ref, left_hi, left_lo, w_hi, w_lo,
    left_f32, right_f32, own_sem, near, left_send, left_recv, right_send, right_recv,
):
    _, kb, rows = left_hbm.shape
    _, kr, cols = right_hbm.shape
    depth = kb * n_col
    chunks = cols // LANES
    line = n_col // 2
    fine = by_slab(kb, kr, line)
    pieces = right_pieces(kb, kr, line, chunks)

    x = lax.axis_index("row")
    place = lax.axis_index("col")
    z, core = place // 2, lax.rem(place, 2)
    has_next, has_prev = z + 1 < line, z >= 1
    leads = core == 0

    def at(zz, cc):
        return {"col": zz * 2 + cc}

    def peer(d):
        return lax.rem(x + d, n_row)

    barrier = pltpu.get_barrier_semaphore()
    for d in range(1, n_row):
        pl.semaphore_signal(barrier, inc=1, device_id={"row": peer(d)}, device_id_type=MESH)

    def tell(sem):
        @pl.when(leads & has_next)
        def _():
            pl.semaphore_signal(sem, inc=1, device_id=at(z + 1, core), device_id_type=MESH)

        @pl.when(leads & has_prev)
        def _():
            pl.semaphore_signal(sem, inc=1, device_id=at(z - 1, core), device_id_type=MESH)

    tell(barrier)

    @pl.when(core == 1)
    def _():
        pl.semaphore_signal(barrier, inc=1, device_id=at(z, 0), device_id_type=MESH)

    own_right = pltpu.make_async_copy(
        right_hbm, right_f32.at[:, pl.ds(pl.multiple_of(x * kr, 8), kr), :], own_sem.at[0])
    own_right.start()
    own_left = pltpu.make_async_copy(
        left_hbm, left_f32.at[:, pl.ds(pl.multiple_of(place * kb, 8), kb), :], own_sem.at[1])
    own_left.start()

    beside = has_next.astype(jnp.int32) + has_prev.astype(jnp.int32)
    pl.semaphore_wait(barrier, n_row - 1 + jnp.where(leads, beside + 1, 0))

    def right_copy(d, q):
        j, first, count = pieces[q]
        span = pl.ds(pl.multiple_of(x * kr + first, 8), count)
        return pltpu.make_async_remote_copy(
            src_ref=right_hbm.at[:, pl.ds(first, count), pl.ds(j * LANES, LANES)],
            dst_ref=right_f32.at[:, span, pl.ds(j * LANES, LANES)],
            send_sem=right_send.at[d - 1, q],
            recv_sem=right_recv.at[d - 1, q],
            device_id={"row": peer(d)},
            device_id_type=MESH,
        )

    def left_slot(zz, cc, part):
        return left_f32.at[part, pl.ds(pl.multiple_of((zz * 2 + cc) * kb, 8), kb), :]

    def left_copy(way, zz, cc, part, target, own=False):
        return pltpu.make_async_remote_copy(
            src_ref=left_hbm.at[part] if own else left_slot(zz, cc, part),
            dst_ref=left_slot(zz, cc, part),
            send_sem=left_send.at[way, zz, part],
            recv_sem=left_recv.at[cc, zz, part],
            device_id=target,
            device_id_type=MESH,
        )

    def up(zz, part, own=False):
        return left_copy(0, zz, core, part, at(z + 1, core), own)

    def down(zz, part, own=False):
        return left_copy(1, zz, core, part, at(z - 1, core), own)

    def across(zz, part, own=False):
        return left_copy(2, zz, core, part, at(z, 1 - core), own)

    def arrived(zz, cc, part):
        left_copy(2, zz, cc, part, at(z, 1 - core)).wait_recv()

    def right_sends():
        for q in range(len(pieces)):
            for d in range(1, n_row):
                right_copy(d, q).start()

    def left_sends():
        for part in range(2):
            @pl.when(has_next)
            def _():
                up(z, part, True).start()

            @pl.when(has_prev)
            def _():
                down(z, part, True).start()
        for part in range(2):
            across(z, part, True).start()

    @pl.when(leads)
    def _():
        tell(near)
        left_sends()
        right_sends()
        pl.semaphore_wait(near, beside)
        pl.semaphore_signal(near, inc=1, device_id=at(z, 1), device_id_type=MESH)

    @pl.when(core == 1)
    def _():
        right_sends()
        pl.semaphore_wait(near, 1)
        left_sends()

    def to_weights(owner, q):
        j, first, count = pieces[q]
        for r in range(first, first + count, min(count, LANES)):
            n = min(count, LANES)
            row = pl.multiple_of(owner * kr + r, n)
            re = split(right_f32[0, pl.ds(row, n), j * LANES:(j + 1) * LANES])
            im = split(right_f32[1, pl.ds(row, n), j * LANES:(j + 1) * LANES])
            base = row + row // LANES * LANES
            above, below = pl.ds(pl.multiple_of(base, n), n), pl.ds(pl.multiple_of(base + LANES, n), n)
            for w, a, b in ((w_hi, re[0], im[0]), (w_lo, re[1], im[1])):
                w[j, above, :LANES] = a
                w[j, above, LANES:] = b
                w[j, below, :LANES] = -b
                w[j, below, LANES:] = a

    def convert(g):
        for part in range(2):
            block = left_f32[part, pl.ds(pl.multiple_of(g * LANES, LANES), LANES), :].T
            high, low = split(block)
            where = pl.ds(pl.multiple_of(g * PAIR + part * LANES, LANES), LANES)
            left_hi[:, where] = high
            left_lo[:, where] = low

    def multiply(j, first, count, add=False):
        span = pl.ds(pl.multiple_of(first, PAIR), count)
        total = three_dots(left_hi[:, span], left_lo[:, span], w_hi[j, span, :], w_lo[j, span, :])
        lanes = slice(j * LANES, (j + 1) * LANES)
        for part in range(2):
            value = total[:, part * LANES:(part + 1) * LANES]
            out_ref[part, :, lanes] = out_ref[part, :, lanes] + value if add else value

    def settle(zz):
        for part in range(2):
            arrived(zz, 1 - core, part)
        if fine:
            convert(zz)

    def settle_at(d):
        if d == 0:
            settle(z)
            return

        @pl.when(z - d >= 0)
        def _():
            settle(z - d)

        @pl.when(z + d < line)
        def _():
            settle(z + d)

    def right_arrived(q):
        for d in range(1, n_row):
            right_copy(d, q).wait_recv()
            to_weights(peer(n_row - d), q)

    def left_sent():
        for part in range(2):
            for d in range(line):
                own = d == 0

                @pl.when(z - d >= 0)
                def _():
                    @pl.when(has_next)
                    def _():
                        up(z - d, part, own).wait_send()

                    across(z - d, part, own).wait_send()

                @pl.when(z + d < line)
                def _():
                    @pl.when(has_prev)
                    def _():
                        down(z + d, part, own).wait_send()

                    if d > 0:
                        across(z + d, part).wait_send()

    own_right.wait()
    for q in range(len(pieces)):
        to_weights(x, q)
    own_left.wait()

    far = jnp.where(2 * z < line, line - 1, 0)
    others = jnp.where(2 * z < line, 0, PAIR)

    def most(j):
        right_arrived(j)
        multiply(j, others, (line - 1) * PAIR)

    early = max(chunks - 2, 0) if fine else 0
    for d in range(1, line):
        if fine and d == line - 1:
            settle_at(d - 1)
            for j in range(early):
                most(j)
        for part in range(2):
            @pl.when(z - d >= 0)
            def _():
                arrived(z - d, core, part)

                @pl.when(has_next)
                def _():
                    up(z - d, part).start()

                across(z - d, part).start()

            @pl.when(z + d < line)
            def _():
                arrived(z + d, core, part)

                @pl.when(has_prev)
                def _():
                    down(z + d, part).start()

                across(z + d, part).start()

        if not (fine and d == line - 1):
            settle_at(d - 1)

    if fine:
        for j in range(early, chunks - 1):
            most(j)
        settle_at(line - 1)
        for j in range(chunks - 1):
            multiply(j, far * PAIR, PAIR, True)
        for i in range(kr // LANES):
            multiply(chunks - 1, (x * (kr // LANES) + i) * PAIR, PAIR, i > 0)
        left_sent()
        for q in range(chunks - 1, len(pieces)):
            for d in range(1, n_row):
                owner = peer(n_row - d)
                right_copy(d, q).wait_recv()
                to_weights(owner, q)
                multiply(chunks - 1, (owner * (kr // LANES) + pieces[q][1] // LANES) * PAIR, PAIR, True)
    else:
        settle_at(line - 1)
        for g in range(depth // LANES):
            convert(g)
        left_sent()
        for j in range(chunks):
            right_arrived(j)
            multiply(j, 0, 2 * depth)

    for q in range(len(pieces)):
        for d in range(1, n_row):
            right_copy(d, q).wait_send()


def body(n_row, n_col, left_data, right_data):
    left = jnp.swapaxes(left_data, 1, 2)
    _, kb, rows = left.shape
    _, kr, cols = right_data.shape
    depth, chunks, line = kb * n_col, cols // LANES, n_col // 2
    n_pieces = len(right_pieces(kb, kr, line, chunks))
    vmem = pl.BlockSpec(memory_space=pltpu.VMEM)
    done = pl.pallas_call(
        functools.partial(kernel, n_row, n_col),
        out_shape=jax.ShapeDtypeStruct((2, rows, cols), jnp.float32),
        in_specs=[pl.BlockSpec(memory_space=pltpu.HBM)] * 2,
        out_specs=vmem,
        scratch_shapes=[
            pltpu.VMEM((rows, 2 * depth), jnp.bfloat16),
            pltpu.VMEM((rows, 2 * depth), jnp.bfloat16),
            pltpu.VMEM((chunks, 2 * depth, PAIR), jnp.bfloat16),
            pltpu.VMEM((chunks, 2 * depth, PAIR), jnp.bfloat16),
            pltpu.VMEM((2, depth, rows), jnp.float32),
            pltpu.VMEM((2, depth, cols), jnp.float32),
            pltpu.SemaphoreType.DMA((2,)),
            pltpu.SemaphoreType.REGULAR,
            pltpu.SemaphoreType.DMA((3, line, 2)),
            pltpu.SemaphoreType.DMA((2, line, 2)),
            pltpu.SemaphoreType.DMA((n_row - 1, n_pieces)),
            pltpu.SemaphoreType.DMA((n_row - 1, n_pieces)),
        ],
        compiler_params=pltpu.CompilerParams(
            collective_id=0, has_side_effects=True, vmem_limit_bytes=32 * 1024 * 1024),
    )(pltpu.with_memory_space_constraint(left, pltpu.HBM), pltpu.with_memory_space_constraint(right_data, pltpu.HBM))
    return pl.pallas_call(
        write,
        out_shape=jax.ShapeDtypeStruct((2, rows, cols), jnp.float32),
        in_specs=[vmem],
        out_specs=pl.BlockSpec(memory_space=pltpu.HBM),
        scratch_shapes=[pltpu.SemaphoreType.DMA((1,))],
        compiler_params=pltpu.CompilerParams(vmem_limit_bytes=16 * 1024 * 1024),
    )(done)


def solution(mesh):
    placed = (P(None, ("freq", "row"), "col"), P(None, "row", ("freq", "col")))
    return jax.shard_map(
        functools.partial(body, mesh.shape["row"], mesh.shape["col"]),
        mesh=mesh, in_specs=placed, out_specs=P(None, ("freq", "row"), "col"), check_vma=False,
    )
```

time: 30.2 us -> 29.1 us (0.964)
  the two profiles are of different devices: /device:TPU:0 before, /device:TPU:1 now
where the time goes in v1:
time: 29.1 us; the launch traced here: 28.6 us
  Pallas kernels  28.5 us (98%)
    pallas_call x1, Pallas kernels, body(): pl.pallas_call(functools.partial(kernel, n_row, n_col), out_shape=jax.Sha...  27.2 us
    pallas_call x1, Pallas kernels, body(): pl.pallas_call(write, out_shape=jax.ShapeDtypeStruct((2, rows, cols), jnp...  1.33 us

profile of v1, /device:TPU:1, one launch (start us, length us, event | category | flops | bytes accessed | tf_op | source)
XLA Modules:
  0.0 28.6 jit_solution(18040180090946549066)
XLA Ops:
  0.0 27.2 %shard_map.28.done_ref = f32[2,512,512]{2,1,0:T(8,128)S(1)} custom-call(f32[2,64,512]{2,1,0:T(8,128)} %bitcast.1, f32[2,256,512]{2,1,0:T(8,128)} %right_hbm.1), custom_call_target="tpu_custom_call" | custom-call | tf_op jit(solution)/shard_map/pallas_call | solution.py:321
  27.2 1.3 %shard_map.29 = f32[2,512,512]{2,1,0:T(8,128)} custom-call(f32[2,512,512]{2,1,0:T(8,128)S(1)} %shard_map.28.done_ref), custom_call_target="tpu_custom_call" | custom-call | tf_op jit(solution)/shard_map/pallas_call | solution.py:343

commit v2 on v1

v2 whole, which is shorter than its diff:
```python
import functools

import jax
import jax.numpy as jnp
from jax import lax
from jax.experimental import pallas as pl
from jax.experimental.pallas import tpu as pltpu
from jax.sharding import PartitionSpec as P

MESH = pl.DeviceIdType.MESH
LANES = 128
PAIR = 2 * LANES


def split(value):
    high = value.astype(jnp.bfloat16)
    return high, (value - high.astype(jnp.float32)).astype(jnp.bfloat16)


def dot(a, b):
    return jnp.dot(a, b, preferred_element_type=jnp.float32)


def three_dots(left_hi, left_lo, w_hi, w_lo):
    return dot(left_hi, w_hi) + (dot(left_hi, w_lo) + dot(left_lo, w_hi))


def by_slab(kb, kr, line):
    return 2 * kb == LANES and kr % LANES == 0 and line > 1


def right_pieces(kb, kr, line, chunks):
    pieces = [(j, 0, kr) for j in range(chunks)]
    if by_slab(kb, kr, line):
        pieces[-1:] = [(chunks - 1, r, LANES) for r in range(0, kr, LANES)]
    return pieces


def finish(
    n_row, step, done_ref, left_hi, left_lo, last_hi, last_lo, out_hbm, tail, sem,
):
    _, rows, cols = done_ref.shape
    if step is None:
        copy = pltpu.make_async_copy(done_ref, out_hbm, sem.at[0])
        copy.start()
        copy.wait()
        return
    groups, offset = step
    ready, half = cols - LANES, rows // 2
    early = pltpu.make_async_copy(
        done_ref.at[:, :, pl.ds(0, ready)], out_hbm.at[:, :, pl.ds(0, ready)], sem.at[0])
    early.start()
    copies = [early]
    x = lax.axis_index("row")
    for i in range(2):
        span = pl.ds(i * half, half)
        total = jnp.concatenate([done_ref[part, span, ready:] for part in range(2)], axis=1)
        for d in range(1, n_row):
            owner = lax.rem(x + n_row - d, n_row)
            where = pl.ds(pl.multiple_of((owner * groups + offset) * PAIR, PAIR), PAIR)
            total += three_dots(left_hi[span, where], left_lo[span, where], last_hi[d - 1], last_lo[d - 1])
        for part in range(2):
            tail[part, span, :] = total[:, part * LANES:(part + 1) * LANES]
        copy = pltpu.make_async_copy(
            tail.at[:, span, :], out_hbm.at[:, span, pl.ds(ready, LANES)], sem.at[1 + i])
        copy.start()
        copies.append(copy)
    for copy in copies:
        copy.wait()


def kernel(
    n_row, n_col, left_hbm, right_hbm, out_ref, left_hi, left_lo, last_hi, last_lo, w_hi, w_lo,
    left_f32, right_f32, own_sem, told, left_send, line_recv, pair_recv, right_send, right_recv,
):
    _, kb, rows = left_hbm.shape
    _, kr, cols = right_hbm.shape
    depth = kb * n_col
    chunks = cols // LANES
    line = n_col // 2
    fine = by_slab(kb, kr, line)
    pieces = right_pieces(kb, kr, line, chunks)

    x = lax.axis_index("row")
    place = lax.axis_index("col")
    z, core = place // 2, lax.rem(place, 2)
    has_next, has_prev = z + 1 < line, z >= 1

    def at(zz, cc):
        return {"col": zz * 2 + cc}

    def peer(d):
        return lax.rem(x + d, n_row)

    def tell(sem, device):
        pl.semaphore_signal(sem, inc=1, device_id=device, device_id_type=MESH)

    barrier = pltpu.get_barrier_semaphore()
    leads = core == 0

    @pl.when(leads & has_next)
    def _():
        tell(barrier, at(z + 1, 0))

    @pl.when(core == 1)
    def _():
        for d in range(1, n_row):
            tell(barrier, {"row": peer(d)})
        tell(barrier, at(z, 0))

    own_right = pltpu.make_async_copy(
        right_hbm, right_f32.at[:, pl.ds(pl.multiple_of(x * kr, 8), kr), :], own_sem.at[0])
    own_right.start()
    own_left = pltpu.make_async_copy(
        left_hbm, left_f32.at[:, pl.ds(pl.multiple_of(place * kb, 8), kb), :], own_sem.at[1])
    own_left.start()

    pl.semaphore_wait(barrier, jnp.where(leads, 1 + has_prev.astype(jnp.int32), n_row - 1))

    def right_copy(d, q):
        j, first, count = pieces[q]
        span = pl.ds(pl.multiple_of(x * kr + first, 8), count)
        return pltpu.make_async_remote_copy(
            src_ref=right_hbm.at[:, pl.ds(first, count), pl.ds(j * LANES, LANES)],
            dst_ref=right_f32.at[:, span, pl.ds(j * LANES, LANES)],
            send_sem=right_send.at[d - 1],
            recv_sem=right_recv.at[d - 1, q],
            device_id={"row": peer(d)},
            device_id_type=MESH,
        )

    def slab(zz, cc):
        return pl.ds(pl.multiple_of((zz * 2 + cc) * kb, 8), kb)

    def left_copy(way, zz, part, target, recv_sem, own):
        here = left_f32.at[part, slab(zz, core), :]
        return pltpu.make_async_remote_copy(
            src_ref=left_hbm.at[part] if own else here,
            dst_ref=here,
            send_sem=left_send.at[way],
            recv_sem=recv_sem,
            device_id=target,
            device_id_type=MESH,
        )

    def up(zz, part, own=False):
        return left_copy(0, zz, part, at(z + 1, core), line_recv.at[zz, part], own)

    def down(zz, part, own=False):
        return left_copy(1, zz, part, at(z - 1, core), line_recv.at[zz, part], own)

    def across(zz, part, own=False):
        return left_copy(2, zz, part, at(z, 1 - core), pair_recv.at[zz], own)

    def whole_copy(ref, send_sem, recv_sem):
        return pltpu.make_async_remote_copy(
            src_ref=ref, dst_ref=ref, send_sem=send_sem, recv_sem=recv_sem,
            device_id=at(z, 1 - core), device_id_type=MESH)

    def arrived(zz, part):
        up(zz, part).wait_recv()

    def pair_arrived(zz):
        whole_copy(left_f32.at[:, slab(zz, 1 - core), :], left_send.at[2], pair_recv.at[zz]).wait_recv()

    held = len(pieces) - 1 if fine else len(pieces)

    def right_sends(first, end):
        for q in range(first, end):
            for d in range(1, n_row):
                right_copy(d, q).start()

    def both(copy):
        for part in range(2):
            copy(z, part, True).start()

    rows_in, above, below = told.at[0], told.at[1], told.at[2]
    other, beside = above, below

    @pl.when(leads)
    def _():
        tell(other, at(z, 1))

        @pl.when(has_prev)
        def _():
            tell(above, at(z - 1, 0))
            both(down)

        both(across)

        @pl.when(has_next)
        def _():
            pl.semaphore_wait(above, 1)
            both(up)
            tell(below, at(z + 1, 0))

        pl.semaphore_wait(rows_in, 1)
        right_sends(0, len(pieces))

        @pl.when(has_prev)
        def _():
            pl.semaphore_wait(below, 1)

        tell(beside, at(z, 1))

    @pl.when(core == 1)
    def _():
        right_sends(0, held)
        pl.semaphore_wait(other, 1)
        for d in range(1, n_row):
            tell(rows_in, {"row": peer(d)})
        both(across)
        pl.semaphore_wait(rows_in, n_row - 1)
        tell(rows_in, at(z, 0))
        pl.semaphore_wait(beside, 1)

        @pl.when(has_next)
        def _():
            both(up)

        @pl.when(has_prev)
        def _():
            both(down)

    def to_weights(owner, q):
        j, first, count = pieces[q]
        for r in range(first, first + count, min(count, LANES)):
            n = min(count, LANES)
            row = pl.multiple_of(owner * kr + r, n)
            re = split(right_f32[0, pl.ds(row, n), j * LANES:(j + 1) * LANES])
            im = split(right_f32[1, pl.ds(row, n), j * LANES:(j + 1) * LANES])
            base = row + row // LANES * LANES
            above, below = pl.ds(pl.multiple_of(base, n), n), pl.ds(pl.multiple_of(base + LANES, n), n)
            for w, a, b in ((w_hi, re[0], im[0]), (w_lo, re[1], im[1])):
                w[j, above, :LANES] = a
                w[j, above, LANES:] = b
                w[j, below, :LANES] = -b
                w[j, below, LANES:] = a

    def arrived_weights(g):
        block = pl.ds(pl.multiple_of(g * LANES, LANES), LANES)
        re, im = (right_f32[part, block, cols - LANES:] for part in range(2))
        return split(jnp.concatenate([jnp.concatenate([re, im], 1), jnp.concatenate([-im, re], 1)], 0))

    def convert(g, part):
        block = left_f32[part, pl.ds(pl.multiple_of(g * LANES, LANES), LANES), :].T
        high, low = split(block)
        where = pl.ds(pl.multiple_of(g * PAIR + part * LANES, LANES), LANES)
        left_hi[:, where] = high
        left_lo[:, where] = low

    def add_to(j, total):
        lanes = slice(j * LANES, (j + 1) * LANES)
        for part in range(2):
            out_ref[part, :, lanes] += total[:, part * LANES:(part + 1) * LANES]

    def multiply(j, first, count, add=False):
        span = pl.ds(pl.multiple_of(first, PAIR), count)
        total = three_dots(left_hi[:, span], left_lo[:, span], w_hi[j, span, :], w_lo[j, span, :])
        lanes = slice(j * LANES, (j + 1) * LANES)
        for part in range(2):
            value = total[:, part * LANES:(part + 1) * LANES]
            out_ref[part, :, lanes] = out_ref[part, :, lanes] + value if add else value

    def settle(d):
        def one(zz):
            pair_arrived(zz)
            if fine:
                for part in range(2):
                    convert(zz, part)

        if d == 0:
            one(z)
            return

        @pl.when(z - d >= 0)
        def _():
            one(z - d)

        @pl.when(z + d < line)
        def _():
            one(z + d)

    def right_wait(q):
        for d in range(1, n_row):
            right_copy(d, q).wait_recv()

    def right_arrived(q, waited=False):
        for d in range(1, n_row):
            if not waited:
                right_copy(d, q).wait_recv()
            to_weights(peer(n_row - d), q)

    def all_sent():
        def slabs(n, way):
            whole_copy(left_f32.at[:, pl.ds(0, n * kb), :], left_send.at[way], pair_recv.at[0]).wait_send()

        for n in range(1, line):
            @pl.when(z + 1 == n)
            def _():
                slabs(n, 0)

            @pl.when(line - z == n)
            def _():
                slabs(n, 1)

        slabs(line, 2)
        for d in range(1, n_row):
            whole_copy(right_hbm, right_send.at[d - 1], pair_recv.at[0]).wait_send()

    own_right.wait()
    for q in range(len(pieces)):
        to_weights(x, q)
    own_left.wait()

    def pass_on(d, part):
        @pl.when(z - d >= 0)
        def _():
            arrived(z - d, part)

            @pl.when(has_next)
            def _():
                up(z - d, part).start()

            across(z - d, part).start()

        @pl.when(z + d < line)
        def _():
            arrived(z + d, part)

            @pl.when(has_prev)
            def _():
                down(z + d, part).start()

            across(z + d, part).start()

    if fine:
        low = 2 * z < line
        far = jnp.where(low, line - 1, 0)
        others = jnp.where(low, 0, PAIR)
        groups = kr // LANES
        last = chunks - 1

        def most(j, waited=False):
            right_arrived(j, waited)
            multiply(j, others, (line - 1) * PAIR)

        def own_part(is_far):
            for i in range(groups):
                g = x * groups + i

                @pl.when((g == far) == is_far)
                def _():
                    multiply(last, g * PAIR, PAIR, True)

        out_ref[:, :, last * LANES:] = jnp.zeros((2, rows, LANES), jnp.float32)
        for d in range(1, line - 1):
            for part in range(2):
                pass_on(d, part)
            settle(d - 1)
        settle(line - 2)
        early = max(last - 1, 0)
        for j in range(early):
            most(j)
        own_part(False)
        pass_on(line - 1, 0)

        @pl.when(core == 1)
        def _():
            for j in range(early, last):
                right_wait(j)
            right_sends(held, len(pieces))

        pass_on(line - 1, 1)

        @pl.when(leads)
        def _():
            for j in range(early, last):
                right_wait(j)

        for j in range(early, last):
            most(j, True)
        settle(line - 1)
        for j in range(last):
            multiply(j, far * PAIR, PAIR, True)
        own_part(True)
        for q in range(last, len(pieces) - 1):
            for d in range(1, n_row):
                owner = peer(n_row - d)
                right_copy(d, q).wait_recv()
                g = owner * groups + pieces[q][1] // LANES
                span = pl.ds(pl.multiple_of(g * PAIR, PAIR), PAIR)
                add_to(last, three_dots(left_hi[:, span], left_lo[:, span], *arrived_weights(g)))
        for d in range(1, n_row):
            right_copy(d, len(pieces) - 1).wait_recv()
            g = peer(n_row - d) * groups + pieces[-1][1] // LANES
            last_hi[d - 1], last_lo[d - 1] = arrived_weights(g)
    else:
        for d in range(1, line):
            for part in range(2):
                pass_on(d, part)
            settle(d - 1)
        settle(line - 1)
        for g in range(depth // LANES):
            for part in range(2):
                convert(g, part)
        for j in range(chunks):
            right_arrived(j)
            multiply(j, 0, 2 * depth)

    all_sent()


def body(n_row, n_col, left_data, right_data):
    left = jnp.swapaxes(left_data, 1, 2)
    _, kb, rows = left.shape
    _, kr, cols = right_data.shape
    depth, chunks, line = kb * n_col, cols // LANES, n_col // 2
    n_pieces = len(right_pieces(kb, kr, line, chunks))
    vmem = pl.BlockSpec(memory_space=pltpu.VMEM)
    fine = by_slab(kb, kr, line)
    held = pl.pallas_call(
        functools.partial(kernel, n_row, n_col),
        out_shape=[
            jax.ShapeDtypeStruct((2, rows, cols), jnp.float32),
            jax.ShapeDtypeStruct((rows, 2 * depth), jnp.bfloat16),
            jax.ShapeDtypeStruct((rows, 2 * depth), jnp.bfloat16),
            jax.ShapeDtypeStruct((n_row - 1, PAIR, PAIR), jnp.bfloat16),
            jax.ShapeDtypeStruct((n_row - 1, PAIR, PAIR), jnp.bfloat16),
        ],
        in_specs=[pl.BlockSpec(memory_space=pltpu.HBM)] * 2,
        out_specs=[vmem] * 5,
        scratch_shapes=[
            pltpu.VMEM((chunks, 2 * depth, PAIR), jnp.bfloat16),
            pltpu.VMEM((chunks, 2 * depth, PAIR), jnp.bfloat16),
            pltpu.VMEM((2, depth, rows), jnp.float32),
            pltpu.VMEM((2, depth, cols), jnp.float32),
            pltpu.SemaphoreType.DMA((2,)),
            pltpu.SemaphoreType.REGULAR((3,)),
            pltpu.SemaphoreType.DMA((3,)),
            pltpu.SemaphoreType.DMA((line, 2)),
            pltpu.SemaphoreType.DMA((line,)),
            pltpu.SemaphoreType.DMA((n_row - 1,)),
            pltpu.SemaphoreType.DMA((n_row - 1, n_pieces)),
        ],
        compiler_params=pltpu.CompilerParams(
            collective_id=0, has_side_effects=True, vmem_limit_bytes=32 * 1024 * 1024),
    )(pltpu.with_memory_space_constraint(left, pltpu.HBM), pltpu.with_memory_space_constraint(right_data, pltpu.HBM))
    return pl.pallas_call(
        functools.partial(finish, n_row, (kr // LANES, kr // LANES - 1) if fine else None),
        out_shape=jax.ShapeDtypeStruct((2, rows, cols), jnp.float32),
        in_specs=[vmem] * 5,
        out_specs=pl.BlockSpec(memory_space=pltpu.HBM),
        scratch_shapes=[pltpu.VMEM((2, rows, LANES), jnp.float32), pltpu.SemaphoreType.DMA((3,))],
        compiler_params=pltpu.CompilerParams(vmem_limit_bytes=16 * 1024 * 1024),
    )(*held)


def solution(mesh):
    placed = (P(None, ("freq", "row"), "col"), P(None, "row", ("freq", "col")))
    return jax.shard_map(
        functools.partial(body, mesh.shape["row"], mesh.shape["col"]),
        mesh=mesh, in_specs=placed, out_specs=P(None, ("freq", "row"), "col"), check_vma=False,
    )
```

time: 29.1 us -> 27.6 us (0.948); the launches traced: 28.6 us -> 27.4 us
  Pallas kernels: 28.5 us -> 27.4 us
    pallas_call x2, Pallas kernels: 28.5 us -> 27.4 us  [the longest x1 26 us: body(): pl.pallas_call(functools.partial(kernel, n_row, n_col), out_shape=[jax.Sh...]
where the time goes in v2:
time: 27.6 us; the launch traced here: 27.4 us
  Pallas kernels  27.4 us (99%)
    pallas_call x1, Pallas kernels, body(): pl.pallas_call(functools.partial(kernel, n_row, n_col), out_shape=[jax.Sh...  26 us
    pallas_call x1, Pallas kernels, body(): pl.pallas_call(functools.partial(finish, n_row, (kr // LANES, kr // LANES...  1.44 us

profile of v2, /device:TPU:1, one launch (start us, length us, event | category | flops | bytes accessed | tf_op | source)
XLA Modules:
  0.0 27.4 jit_solution(8301395815309934460)
XLA Ops:
  0.0 26.0 %shard_map.28 = (f32[2,512,512]{2,1,0:T(8,128)S(1)}, bf16[512,1024]{1,0:T(8,128)(2,1)S(1)}, bf16[512,1024]{1,0:T(8,128)(2,1)S(1)}, bf16[1,256,256]{2,1,0:T(8,128)(2,1)S(1)}, bf16[1,256,256]{2,1,0:T(8,128)(2,1)S(1)}) custom-call(f32[2,64,512]{2,1,0:T(8,128)} %bitcast.1, f32[2,256,512]{2,1,0:T(8,128)} %right_hbm.1), custom_call_target="tpu_custom_call" | custom-call | tf_op jit(solution)/shard_map/pallas_call | solution.py:422
  26.0 1.4 %shard_map.29 = f32[2,512,512]{2,1,0:T(8,128)} custom-call(f32[2,512,512]{2,1,0:T(8,128)S(1)} %get-tuple-element.10.done_ref, bf16[512,1024]{1,0:T(8,128)(2,1)S(1)} %get-tuple-element.11.left_hi, bf16[512,1024]{1,0:T(8,128)(2,1)S(1)} %get-tuple-element.12.left_lo, bf16[1,256,256]{2,1,0:T(8,128)(2,1)S(1)} %get-tuple-element.13.last_hi, ...), custom_call_target="tpu_custom_call" | custom-call | tf_op jit(solution)/shard_map/pallas_call | solution.py:449

commit v3 on v2

--- a/solution.py
+++ b/solution.py
@@ -46,27 +46,22 @@
         copy.wait()
         return
     groups, offset = step
-    ready, half = cols - LANES, rows // 2
+    ready = cols - LANES
     early = pltpu.make_async_copy(
         done_ref.at[:, :, pl.ds(0, ready)], out_hbm.at[:, :, pl.ds(0, ready)], sem.at[0])
     early.start()
-    copies = [early]
     x = lax.axis_index("row")
-    for i in range(2):
-        span = pl.ds(i * half, half)
-        total = jnp.concatenate([done_ref[part, span, ready:] for part in range(2)], axis=1)
-        for d in range(1, n_row):
-            owner = lax.rem(x + n_row - d, n_row)
-            where = pl.ds(pl.multiple_of((owner * groups + offset) * PAIR, PAIR), PAIR)
-            total += three_dots(left_hi[span, where], left_lo[span, where], last_hi[d - 1], last_lo[d - 1])
-        for part in range(2):
-            tail[part, span, :] = total[:, part * LANES:(part + 1) * LANES]
-        copy = pltpu.make_async_copy(
-            tail.at[:, span, :], out_hbm.at[:, span, pl.ds(ready, LANES)], sem.at[1 + i])
-        copy.start()
-        copies.append(copy)
-    for copy in copies:
-        copy.wait()
+    total = jnp.concatenate([done_ref[part, :, ready:] for part in range(2)], axis=1)
+    for d in range(1, n_row):
+        owner = lax.rem(x + n_row - d, n_row)
+        where = pl.ds(pl.multiple_of((owner * groups + offset) * PAIR, PAIR), PAIR)
+        total += three_dots(left_hi[:, where], left_lo[:, where], last_hi[d - 1], last_lo[d - 1])
+    for part in range(2):
+        tail[part] = total[:, part * LANES:(part + 1) * LANES]
+    late = pltpu.make_async_copy(tail, out_hbm.at[:, :, pl.ds(ready, LANES)], sem.at[1])
+    late.start()
+    early.wait()
+    late.wait()
 
 
 def kernel(
@@ -144,10 +139,10 @@
         )
 
     def up(zz, part, own=False):
-        return left_copy(0, zz, part, at(z + 1, core), line_recv.at[zz, part], own)
+        return left_copy(0, zz, part, at(z + 1, core), line_recv.at[lax.rem(zz - z - 2 + 2 * line, line), part], own)
 
     def down(zz, part, own=False):
-        return left_copy(1, zz, part, at(z - 1, core), line_recv.at[zz, part], own)
+        return left_copy(1, zz, part, at(z - 1, core), line_recv.at[lax.rem(zz - z + line, line), part], own)
 
     def across(zz, part, own=False):
         return left_copy(2, zz, part, at(z, 1 - core), pair_recv.at[zz], own)
@@ -158,7 +153,8 @@
             device_id=at(z, 1 - core), device_id_type=MESH)
 
     def arrived(zz, part):
-        up(zz, part).wait_recv()
+        here = left_f32.at[part, slab(zz, core), :]
+        whole_copy(here, left_send.at[2], line_recv.at[lax.rem(zz - z - 1 + line, line), part]).wait_recv()
 
     def pair_arrived(zz):
         whole_copy(left_f32.at[:, slab(zz, 1 - core), :], left_send.at[2], pair_recv.at[zz]).wait_recv()
@@ -438,7 +434,7 @@
             pltpu.SemaphoreType.DMA((2,)),
             pltpu.SemaphoreType.REGULAR((3,)),
             pltpu.SemaphoreType.DMA((3,)),
-            pltpu.SemaphoreType.DMA((line, 2)),
+            pltpu.SemaphoreType.DMA((line - 1, 2)),
             pltpu.SemaphoreType.DMA((line,)),
             pltpu.SemaphoreType.DMA((n_row - 1,)),
             pltpu.SemaphoreType.DMA((n_row - 1, n_pieces)),
@@ -451,7 +447,7 @@
         out_shape=jax.ShapeDtypeStruct((2, rows, cols), jnp.float32),
         in_specs=[vmem] * 5,
         out_specs=pl.BlockSpec(memory_space=pltpu.HBM),
-        scratch_shapes=[pltpu.VMEM((2, rows, LANES), jnp.float32), pltpu.SemaphoreType.DMA((3,))],
+        scratch_shapes=[pltpu.VMEM((2, rows, LANES), jnp.float32), pltpu.SemaphoreType.DMA((2,))],
         compiler_params=pltpu.CompilerParams(vmem_limit_bytes=16 * 1024 * 1024),
     )(*held)
 

time: 27.6 us -> 27.5 us (level)
  no operation moved by 1% of the time
where the time goes in v3:
time: 27.5 us; the launch traced here: 27.3 us
  Pallas kernels  27.3 us (99%)
    pallas_call x1, Pallas kernels, body(): pl.pallas_call(functools.partial(kernel, n_row, n_col), out_shape=[jax.Sh...  26 us
    pallas_call x1, Pallas kernels, body(): pl.pallas_call(functools.partial(finish, n_row, (kr // LANES, kr // LANES...  1.35 us

profile of v3, /device:TPU:1, one launch (start us, length us, event | category | flops | bytes accessed | tf_op | source)
XLA Modules:
  0.0 27.3 jit_solution(14355025139378191090)
XLA Ops:
  0.0 26.0 %shard_map.28 = (f32[2,512,512]{2,1,0:T(8,128)S(1)}, bf16[512,1024]{1,0:T(8,128)(2,1)S(1)}, bf16[512,1024]{1,0:T(8,128)(2,1)S(1)}, bf16[1,256,256]{2,1,0:T(8,128)(2,1)S(1)}, bf16[1,256,256]{2,1,0:T(8,128)(2,1)S(1)}) custom-call(f32[2,64,512]{2,1,0:T(8,128)} %bitcast.1, f32[2,256,512]{2,1,0:T(8,128)} %right_hbm.1), custom_call_target="tpu_custom_call" | custom-call | tf_op jit(solution)/shard_map/pallas_call | solution.py:418
  26.0 1.3 %shard_map.29 = f32[2,512,512]{2,1,0:T(8,128)} custom-call(f32[2,512,512]{2,1,0:T(8,128)S(1)} %get-tuple-element.10.done_ref, bf16[512,1024]{1,0:T(8,128)(2,1)S(1)} %get-tuple-element.11.left_hi, bf16[512,1024]{1,0:T(8,128)(2,1)S(1)} %get-tuple-element.12.left_lo, bf16[1,256,256]{2,1,0:T(8,128)(2,1)S(1)} %get-tuple-element.13.last_hi, ...), custom_call_target="tpu_custom_call" | custom-call | tf_op jit(solution)/shard_map/pallas_call | solution.py:445

commit v4 on v3

--- a/solution.py
+++ b/solution.py
@@ -97,10 +97,15 @@
     def _():
         tell(barrier, at(z + 1, 0))
 
-    @pl.when(core == 1)
+    direct = (core == 1) | (z == 0)
+
+    @pl.when(direct)
     def _():
         for d in range(1, n_row):
             tell(barrier, {"row": peer(d)})
+
+    @pl.when(core == 1)
+    def _():
         tell(barrier, at(z, 0))
 
     own_right = pltpu.make_async_copy(
@@ -110,7 +115,7 @@
         left_hbm, left_f32.at[:, pl.ds(pl.multiple_of(place * kb, 8), kb), :], own_sem.at[1])
     own_left.start()
 
-    pl.semaphore_wait(barrier, jnp.where(leads, 1 + has_prev.astype(jnp.int32), n_row - 1))
+    pl.semaphore_wait(barrier, jnp.where(direct, n_row - 1, 0) + jnp.where(leads, 1 + has_prev.astype(jnp.int32), 0))
 
     def right_copy(d, q):
         j, first, count = pieces[q]
@@ -159,7 +164,7 @@
     def pair_arrived(zz):
         whole_copy(left_f32.at[:, slab(zz, 1 - core), :], left_send.at[2], pair_recv.at[zz]).wait_recv()
 
-    held = len(pieces) - 1 if fine else len(pieces)
+    held = 1 if fine and line > 2 else len(pieces)
 
     def right_sends(first, end):
         for q in range(first, end):
@@ -175,6 +180,10 @@
 
     @pl.when(leads)
     def _():
+        @pl.when(z == 0)
+        def _():
+            right_sends(0, len(pieces))
+
         tell(other, at(z, 1))
 
         @pl.when(has_prev)
@@ -190,11 +199,10 @@
             both(up)
             tell(below, at(z + 1, 0))
 
-        pl.semaphore_wait(rows_in, 1)
-        right_sends(0, len(pieces))
-
         @pl.when(has_prev)
         def _():
+            pl.semaphore_wait(rows_in, 1)
+            right_sends(0, len(pieces))
             pl.semaphore_wait(below, 1)
 
         tell(beside, at(z, 1))
@@ -203,11 +211,18 @@
     def _():
         right_sends(0, held)
         pl.semaphore_wait(other, 1)
-        for d in range(1, n_row):
-            tell(rows_in, {"row": peer(d)})
+        @pl.when(has_prev)
+        def _():
+            for d in range(1, n_row):
+                tell(rows_in, {"row": peer(d)})
+
         both(across)
-        pl.semaphore_wait(rows_in, n_row - 1)
-        tell(rows_in, at(z, 0))
+
+        @pl.when(has_prev)
+        def _():
+            pl.semaphore_wait(rows_in, n_row - 1)
+            tell(rows_in, at(z, 0))
+
         pl.semaphore_wait(beside, 1)
 
         @pl.when(has_next)
@@ -277,14 +292,9 @@
         def _():
             one(z + d)
 
-    def right_wait(q):
+    def right_arrived(q):
         for d in range(1, n_row):
             right_copy(d, q).wait_recv()
-
-    def right_arrived(q, waited=False):
-        for d in range(1, n_row):
-            if not waited:
-                right_copy(d, q).wait_recv()
             to_weights(peer(n_row - d), q)
 
     def all_sent():
@@ -337,8 +347,8 @@
         groups = kr // LANES
         last = chunks - 1
 
-        def most(j, waited=False):
-            right_arrived(j, waited)
+        def most(j):
+            right_arrived(j)
             multiply(j, others, (line - 1) * PAIR)
 
         def own_part(is_far):
@@ -353,6 +363,11 @@
         for d in range(1, line - 1):
             for part in range(2):
                 pass_on(d, part)
+                if d == 1 and part == 0:
+                    @pl.when(core == 1)
+                    def _():
+                        right_sends(held, len(pieces))
+
             settle(d - 1)
         settle(line - 2)
         early = max(last - 1, 0)
@@ -361,21 +376,9 @@
         own_part(False)
         pass_on(line - 1, 0)
 
-        @pl.when(core == 1)
-        def _():
-            for j in range(early, last):
-                right_wait(j)
-            right_sends(held, len(pieces))
-
         pass_on(line - 1, 1)
-
-        @pl.when(leads)
-        def _():
-            for j in range(early, last):
-                right_wait(j)
-
         for j in range(early, last):
-            most(j, True)
+            most(j)
         settle(line - 1)
         for j in range(last):
             multiply(j, far * PAIR, PAIR, True)

time: 27.5 us -> 27.5 us (level)
  no operation moved by 1% of the time
where the time goes in v4:
time: 27.5 us; the launch traced here: 27.3 us
  Pallas kernels  27.3 us (99%)
    pallas_call x1, Pallas kernels, body(): pl.pallas_call(functools.partial(kernel, n_row, n_col), out_shape=[jax.Sh...  26 us
    pallas_call x1, Pallas kernels, body(): pl.pallas_call(functools.partial(finish, n_row, (kr // LANES, kr // LANES...  1.35 us

profile of v4, /device:TPU:1, one launch (start us, length us, event | category | flops | bytes accessed | tf_op | source)
XLA Modules:
  0.0 27.3 jit_solution(4385565820881410599)
XLA Ops:
  0.0 26.0 %shard_map.28 = (f32[2,512,512]{2,1,0:T(8,128)S(1)}, bf16[512,1024]{1,0:T(8,128)(2,1)S(1)}, bf16[512,1024]{1,0:T(8,128)(2,1)S(1)}, bf16[1,256,256]{2,1,0:T(8,128)(2,1)S(1)}, bf16[1,256,256]{2,1,0:T(8,128)(2,1)S(1)}) custom-call(f32[2,64,512]{2,1,0:T(8,128)} %bitcast.1, f32[2,256,512]{2,1,0:T(8,128)} %right_hbm.1), custom_call_target="tpu_custom_call" | custom-call | tf_op jit(solution)/shard_map/pallas_call | solution.py:421
  26.0 1.3 %shard_map.29 = f32[2,512,512]{2,1,0:T(8,128)} custom-call(f32[2,512,512]{2,1,0:T(8,128)S(1)} %get-tuple-element.10.done_ref, bf16[512,1024]{1,0:T(8,128)(2,1)S(1)} %get-tuple-element.11.left_hi, bf16[512,1024]{1,0:T(8,128)(2,1)S(1)} %get-tuple-element.12.left_lo, bf16[1,256,256]{2,1,0:T(8,128)(2,1)S(1)} %get-tuple-element.13.last_hi, ...), custom_call_target="tpu_custom_call" | custom-call | tf_op jit(solution)/shard_map/pallas_call | solution.py:448

commit v5 on v4

--- a/solution.py
+++ b/solution.py
@@ -117,6 +117,8 @@
 
     pl.semaphore_wait(barrier, jnp.where(direct, n_row - 1, 0) + jnp.where(leads, 1 + has_prev.astype(jnp.int32), 0))
 
+    paired = fine and chunks > 2
+
     def right_copy(d, q):
         j, first, count = pieces[q]
         span = pl.ds(pl.multiple_of(x * kr + first, 8), count)
@@ -124,7 +126,7 @@
             src_ref=right_hbm.at[:, pl.ds(first, count), pl.ds(j * LANES, LANES)],
             dst_ref=right_f32.at[:, span, pl.ds(j * LANES, LANES)],
             send_sem=right_send.at[d - 1],
-            recv_sem=right_recv.at[d - 1, q],
+            recv_sem=right_recv.at[d - 1, q - 1 if paired and q else q],
             device_id={"row": peer(d)},
             device_id_type=MESH,
         )
@@ -147,10 +149,10 @@
         return left_copy(0, zz, part, at(z + 1, core), line_recv.at[lax.rem(zz - z - 2 + 2 * line, line), part], own)
 
     def down(zz, part, own=False):
-        return left_copy(1, zz, part, at(z - 1, core), line_recv.at[lax.rem(zz - z + line, line), part], own)
+        return left_copy(0, zz, part, at(z - 1, core), line_recv.at[lax.rem(zz - z + line, line), part], own)
 
     def across(zz, part, own=False):
-        return left_copy(2, zz, part, at(z, 1 - core), pair_recv.at[zz], own)
+        return left_copy(1, zz, part, at(z, 1 - core), pair_recv.at[zz], own)
 
     def whole_copy(ref, send_sem, recv_sem):
         return pltpu.make_async_remote_copy(
@@ -159,10 +161,10 @@
 
     def arrived(zz, part):
         here = left_f32.at[part, slab(zz, core), :]
-        whole_copy(here, left_send.at[2], line_recv.at[lax.rem(zz - z - 1 + line, line), part]).wait_recv()
+        whole_copy(here, left_send.at[1], line_recv.at[lax.rem(zz - z - 1 + line, line), part]).wait_recv()
 
     def pair_arrived(zz):
-        whole_copy(left_f32.at[:, slab(zz, 1 - core), :], left_send.at[2], pair_recv.at[zz]).wait_recv()
+        whole_copy(left_f32.at[:, slab(zz, 1 - core), :], left_send.at[1], pair_recv.at[zz]).wait_recv()
 
     held = 1 if fine and line > 2 else len(pieces)
 
@@ -294,23 +296,31 @@
 
     def right_arrived(q):
         for d in range(1, n_row):
-            right_copy(d, q).wait_recv()
+            if not paired or q > 1:
+                right_copy(d, q).wait_recv()
+            elif q == 0:
+                both_here = right_f32.at[:, pl.ds(0, kr), pl.ds(0, 2 * LANES)]
+                whole_copy(both_here, left_send.at[1], right_recv.at[d - 1, 0]).wait_recv()
             to_weights(peer(n_row - d), q)
 
-    def all_sent():
+    def left_sent():
         def slabs(n, way):
             whole_copy(left_f32.at[:, pl.ds(0, n * kb), :], left_send.at[way], pair_recv.at[0]).wait_send()
 
-        for n in range(1, line):
-            @pl.when(z + 1 == n)
+        if line > 1:
+            between = has_next & has_prev
+
+            @pl.when(between)
             def _():
-                slabs(n, 0)
-
-            @pl.when(line - z == n)
+                slabs(line + 1, 0)
+
+            @pl.when(~between)
             def _():
-                slabs(n, 1)
-
-        slabs(line, 2)
+                slabs(1, 0)
+
+        slabs(line, 1)
+
+    def right_sent():
         for d in range(1, n_row):
             whole_copy(right_hbm, right_send.at[d - 1], pair_recv.at[0]).wait_send()
 
@@ -390,6 +400,7 @@
                 g = owner * groups + pieces[q][1] // LANES
                 span = pl.ds(pl.multiple_of(g * PAIR, PAIR), PAIR)
                 add_to(last, three_dots(left_hi[:, span], left_lo[:, span], *arrived_weights(g)))
+        left_sent()
         for d in range(1, n_row):
             right_copy(d, len(pieces) - 1).wait_recv()
             g = peer(n_row - d) * groups + pieces[-1][1] // LANES
@@ -406,8 +417,9 @@
         for j in range(chunks):
             right_arrived(j)
             multiply(j, 0, 2 * depth)
-
-    all_sent()
+        left_sent()
+
+    right_sent()
 
 
 def body(n_row, n_col, left_data, right_data):
@@ -436,11 +448,11 @@
             pltpu.VMEM((2, depth, cols), jnp.float32),
             pltpu.SemaphoreType.DMA((2,)),
             pltpu.SemaphoreType.REGULAR((3,)),
-            pltpu.SemaphoreType.DMA((3,)),
+            pltpu.SemaphoreType.DMA((2,)),
             pltpu.SemaphoreType.DMA((line - 1, 2)),
             pltpu.SemaphoreType.DMA((line,)),
             pltpu.SemaphoreType.DMA((n_row - 1,)),
-            pltpu.SemaphoreType.DMA((n_row - 1, n_pieces)),
+            pltpu.SemaphoreType.DMA((n_row - 1, n_pieces - (fine and chunks > 2))),
         ],
         compiler_params=pltpu.CompilerParams(
             collective_id=0, has_side_effects=True, vmem_limit_bytes=32 * 1024 * 1024),

time: 27.5 us -> 27.4 us (level)
  no operation moved by 1% of the time
where the time goes in v5:
time: 27.4 us; the launch traced here: 27.3 us
  Pallas kernels  27.3 us (100%)
    pallas_call x1, Pallas kernels, body(): pl.pallas_call(functools.partial(kernel, n_row, n_col), out_shape=[jax.Sh...  25.9 us
    pallas_call x1, Pallas kernels, body(): pl.pallas_call(functools.partial(finish, n_row, (kr // LANES, kr // LANES...  1.35 us

profile of v5, /device:TPU:1, one launch (start us, length us, event | category | flops | bytes accessed | tf_op | source)
XLA Modules:
  0.0 27.3 jit_solution(5603076516904083766)
XLA Ops:
  0.0 25.9 %shard_map.28 = (f32[2,512,512]{2,1,0:T(8,128)S(1)}, bf16[512,1024]{1,0:T(8,128)(2,1)S(1)}, bf16[512,1024]{1,0:T(8,128)(2,1)S(1)}, bf16[1,256,256]{2,1,0:T(8,128)(2,1)S(1)}, bf16[1,256,256]{2,1,0:T(8,128)(2,1)S(1)}) custom-call(f32[2,64,512]{2,1,0:T(8,128)} %bitcast.1, f32[2,256,512]{2,1,0:T(8,128)} %right_hbm.1), custom_call_target="tpu_custom_call" | custom-call | tf_op jit(solution)/shard_map/pallas_call | solution.py:433
  26.0 1.3 %shard_map.29 = f32[2,512,512]{2,1,0:T(8,128)} custom-call(f32[2,512,512]{2,1,0:T(8,128)S(1)} %get-tuple-element.10.done_ref, bf16[512,1024]{1,0:T(8,128)(2,1)S(1)} %get-tuple-element.11.left_hi, bf16[512,1024]{1,0:T(8,128)(2,1)S(1)} %get-tuple-element.12.left_lo, bf16[1,256,256]{2,1,0:T(8,128)(2,1)S(1)} %get-tuple-element.13.last_hi, ...), custom_call_target="tpu_custom_call" | custom-call | tf_op jit(solution)/shard_map/pallas_call | solution.py:460

commit v6 on v5

--- a/solution.py
+++ b/solution.py
@@ -25,6 +25,10 @@
     return dot(left_hi, w_hi) + (dot(left_hi, w_lo) + dot(left_lo, w_hi))
 
 
+def weights(re, im):
+    return split(jnp.concatenate([jnp.concatenate([re, im], 1), jnp.concatenate([-im, re], 1)], 0))
+
+
 def by_slab(kb, kr, line):
     return 2 * kb == LANES and kr % LANES == 0 and line > 1
 
@@ -37,7 +41,7 @@
 
 
 def finish(
-    n_row, step, done_ref, left_hi, left_lo, last_hi, last_lo, out_hbm, tail, sem,
+    n_row, step, done_ref, left_hi, left_lo, last_block, out_hbm, tail, sem,
 ):
     _, rows, cols = done_ref.shape
     if step is None:
@@ -55,7 +59,8 @@
     for d in range(1, n_row):
         owner = lax.rem(x + n_row - d, n_row)
         where = pl.ds(pl.multiple_of((owner * groups + offset) * PAIR, PAIR), PAIR)
-        total += three_dots(left_hi[:, where], left_lo[:, where], last_hi[d - 1], last_lo[d - 1])
+        total += three_dots(
+            left_hi[:, where], left_lo[:, where], *weights(last_block[d - 1, 0], last_block[d - 1, 1]))
     for part in range(2):
         tail[part] = total[:, part * LANES:(part + 1) * LANES]
     late = pltpu.make_async_copy(tail, out_hbm.at[:, :, pl.ds(ready, LANES)], sem.at[1])
@@ -65,7 +70,7 @@
 
 
 def kernel(
-    n_row, n_col, left_hbm, right_hbm, out_ref, left_hi, left_lo, last_hi, last_lo, w_hi, w_lo,
+    n_row, n_col, left_hbm, right_hbm, out_ref, left_hi, left_lo, last_block, w_hi, w_lo,
     left_f32, right_f32, own_sem, told, left_send, line_recv, pair_recv, right_send, right_recv,
 ):
     _, kb, rows = left_hbm.shape
@@ -250,10 +255,8 @@
                 w[j, below, :LANES] = -b
                 w[j, below, LANES:] = a
 
-    def arrived_weights(g):
-        block = pl.ds(pl.multiple_of(g * LANES, LANES), LANES)
-        re, im = (right_f32[part, block, cols - LANES:] for part in range(2))
-        return split(jnp.concatenate([jnp.concatenate([re, im], 1), jnp.concatenate([-im, re], 1)], 0))
+    def arrived_block(g, part):
+        return right_f32[part, pl.ds(pl.multiple_of(g * LANES, LANES), LANES), cols - LANES:]
 
     def convert(g, part):
         block = left_f32[part, pl.ds(pl.multiple_of(g * LANES, LANES), LANES), :].T
@@ -399,12 +402,13 @@
                 right_copy(d, q).wait_recv()
                 g = owner * groups + pieces[q][1] // LANES
                 span = pl.ds(pl.multiple_of(g * PAIR, PAIR), PAIR)
-                add_to(last, three_dots(left_hi[:, span], left_lo[:, span], *arrived_weights(g)))
+                add_to(last, three_dots(left_hi[:, span], left_lo[:, span], *weights(arrived_block(g, 0), arrived_block(g, 1))))
         left_sent()
         for d in range(1, n_row):
             right_copy(d, len(pieces) - 1).wait_recv()
             g = peer(n_row - d) * groups + pieces[-1][1] // LANES
-            last_hi[d - 1], last_lo[d - 1] = arrived_weights(g)
+            for part in range(2):
+                last_block[d - 1, part] = arrived_block(g, part)
     else:
         for d in range(1, line):
             for part in range(2):
@@ -436,11 +440,10 @@
             jax.ShapeDtypeStruct((2, rows, cols), jnp.float32),
             jax.ShapeDtypeStruct((rows, 2 * depth), jnp.bfloat16),
             jax.ShapeDtypeStruct((rows, 2 * depth), jnp.bfloat16),
-            jax.ShapeDtypeStruct((n_row - 1, PAIR, PAIR), jnp.bfloat16),
-            jax.ShapeDtypeStruct((n_row - 1, PAIR, PAIR), jnp.bfloat16),
+            jax.ShapeDtypeStruct((n_row - 1, 2, LANES, LANES), jnp.float32),
         ],
         in_specs=[pl.BlockSpec(memory_space=pltpu.HBM)] * 2,
-        out_specs=[vmem] * 5,
+        out_specs=[vmem] * 4,
         scratch_shapes=[
             pltpu.VMEM((chunks, 2 * depth, PAIR), jnp.bfloat16),
             pltpu.VMEM((chunks, 2 * depth, PAIR), jnp.bfloat16),
@@ -460,7 +463,7 @@
     return pl.pallas_call(
         functools.partial(finish, n_row, (kr // LANES, kr // LANES - 1) if fine else None),
         out_shape=jax.ShapeDtypeStruct((2, rows, cols), jnp.float32),
-        in_specs=[vmem] * 5,
+        in_specs=[vmem] * 4,
         out_specs=pl.BlockSpec(memory_space=pltpu.HBM),
         scratch_shapes=[pltpu.VMEM((2, rows, LANES), jnp.float32), pltpu.SemaphoreType.DMA((2,))],
         compiler_params=pltpu.CompilerParams(vmem_limit_bytes=16 * 1024 * 1024),

time: 27.4 us -> 27.4 us (level)
  no operation moved by 1% of the time
where the time goes in v6:
time: 27.4 us; the launch traced here: 27.3 us
  Pallas kernels  27.3 us (100%)
    pallas_call x1, Pallas kernels, body(): pl.pallas_call(functools.partial(kernel, n_row, n_col), out_shape=[jax.Sh...  25.9 us
    pallas_call x1, Pallas kernels, body(): pl.pallas_call(functools.partial(finish, n_row, (kr // LANES, kr // LANES...  1.34 us

profile of v6, /device:TPU:1, one launch (start us, length us, event | category | flops | bytes accessed | tf_op | source)
XLA Modules:
  0.0 27.3 jit_solution(15907419500926778776)
XLA Ops:
  0.0 25.9 %shard_map.28 = (f32[2,512,512]{2,1,0:T(8,128)S(1)}, bf16[512,1024]{1,0:T(8,128)(2,1)S(1)}, bf16[512,1024]{1,0:T(8,128)(2,1)S(1)}, f32[1,2,128,128]{3,2,1,0:T(8,128)S(1)}) custom-call(f32[2,64,512]{2,1,0:T(8,128)} %bitcast.1, f32[2,256,512]{2,1,0:T(8,128)} %right_hbm.1), custom_call_target="tpu_custom_call" | custom-call | tf_op jit(solution)/shard_map/pallas_call | solution.py:437
  25.9 1.3 %shard_map.29 = f32[2,512,512]{2,1,0:T(8,128)} custom-call(f32[2,512,512]{2,1,0:T(8,128)S(1)} %get-tuple-element.9.done_ref, bf16[512,1024]{1,0:T(8,128)(2,1)S(1)} %get-tuple-element.10.left_hi, bf16[512,1024]{1,0:T(8,128)(2,1)S(1)} %get-tuple-element.11.left_lo, f32[1,2,128,128]{3,2,1,0:T(8,128)S(1)} %get-tuple-element.12.last_block), custom_call_target="tpu_custom_call" | custom-call | tf_op jit(solution)/shard_map/pallas_call | solution.py:463

commit v7 on v6

--- a/solution.py
+++ b/solution.py
@@ -115,10 +115,8 @@
 
     own_right = pltpu.make_async_copy(
         right_hbm, right_f32.at[:, pl.ds(pl.multiple_of(x * kr, 8), kr), :], own_sem.at[0])
-    own_right.start()
     own_left = pltpu.make_async_copy(
         left_hbm, left_f32.at[:, pl.ds(pl.multiple_of(place * kb, 8), kb), :], own_sem.at[1])
-    own_left.start()
 
     pl.semaphore_wait(barrier, jnp.where(direct, n_row - 1, 0) + jnp.where(leads, 1 + has_prev.astype(jnp.int32), 0))
 
@@ -187,6 +185,9 @@
 
     @pl.when(leads)
     def _():
+        own_right.start()
+        own_left.start()
+
         @pl.when(z == 0)
         def _():
             right_sends(0, len(pieces))
@@ -217,6 +218,8 @@
     @pl.when(core == 1)
     def _():
         right_sends(0, held)
+        own_right.start()
+        own_left.start()
         pl.semaphore_wait(other, 1)
         @pl.when(has_prev)
         def _():

time: 27.4 us -> 27.4 us (level)
  no operation moved by 1% of the time
where the time goes in v7:
time: 27.4 us; the launch traced here: 27.2 us
  Pallas kernels  27.2 us (99%)
    pallas_call x1, Pallas kernels, body(): pl.pallas_call(functools.partial(kernel, n_row, n_col), out_shape=[jax.Sh...  25.9 us
    pallas_call x1, Pallas kernels, body(): pl.pallas_call(functools.partial(finish, n_row, (kr // LANES, kr // LANES...  1.34 us

profile of v7, /device:TPU:1, one launch (start us, length us, event | category | flops | bytes accessed | tf_op | source)
XLA Modules:
  0.0 27.2 jit_solution(3787528494624152638)
XLA Ops:
  0.0 25.9 %shard_map.28 = (f32[2,512,512]{2,1,0:T(8,128)S(1)}, bf16[512,1024]{1,0:T(8,128)(2,1)S(1)}, bf16[512,1024]{1,0:T(8,128)(2,1)S(1)}, f32[1,2,128,128]{3,2,1,0:T(8,128)S(1)}) custom-call(f32[2,64,512]{2,1,0:T(8,128)} %bitcast.1, f32[2,256,512]{2,1,0:T(8,128)} %right_hbm.1), custom_call_target="tpu_custom_call" | custom-call | tf_op jit(solution)/shard_map/pallas_call | solution.py:440
  25.9 1.3 %shard_map.29 = f32[2,512,512]{2,1,0:T(8,128)} custom-call(f32[2,512,512]{2,1,0:T(8,128)S(1)} %get-tuple-element.9.done_ref, bf16[512,1024]{1,0:T(8,128)(2,1)S(1)} %get-tuple-element.10.left_hi, bf16[512,1024]{1,0:T(8,128)(2,1)S(1)} %get-tuple-element.11.left_lo, f32[1,2,128,128]{3,2,1,0:T(8,128)S(1)} %get-tuple-element.12.last_block), custom_call_target="tpu_custom_call" | custom-call | tf_op jit(solution)/shard_map/pallas_call | solution.py:466

commit v8 on v7

--- a/solution.py
+++ b/solution.py
@@ -379,7 +379,7 @@
         for d in range(1, line - 1):
             for part in range(2):
                 pass_on(d, part)
-                if d == 1 and part == 0:
+                if d == 1 and part == 1:
                     @pl.when(core == 1)
                     def _():
                         right_sends(held, len(pieces))

time: 27.4 us -> 27.4 us (level)
  no operation moved by 1% of the time
where the time goes in v8:
time: 27.4 us; the launch traced here: 27.2 us
  Pallas kernels  27.2 us (99%)
    pallas_call x1, Pallas kernels, body(): pl.pallas_call(functools.partial(kernel, n_row, n_col), out_shape=[jax.Sh...  25.9 us
    pallas_call x1, Pallas kernels, body(): pl.pallas_call(functools.partial(finish, n_row, (kr // LANES, kr // LANES...  1.34 us

profile of v8, /device:TPU:1, one launch (start us, length us, event | category | flops | bytes accessed | tf_op | source)
XLA Modules:
  0.0 27.2 jit_solution(9133506424899066302)
XLA Ops:
  0.0 25.9 %shard_map.28 = (f32[2,512,512]{2,1,0:T(8,128)S(1)}, bf16[512,1024]{1,0:T(8,128)(2,1)S(1)}, bf16[512,1024]{1,0:T(8,128)(2,1)S(1)}, f32[1,2,128,128]{3,2,1,0:T(8,128)S(1)}) custom-call(f32[2,64,512]{2,1,0:T(8,128)} %bitcast.1, f32[2,256,512]{2,1,0:T(8,128)} %right_hbm.1), custom_call_target="tpu_custom_call" | custom-call | tf_op jit(solution)/shard_map/pallas_call | solution.py:440
  25.9 1.3 %shard_map.29 = f32[2,512,512]{2,1,0:T(8,128)} custom-call(f32[2,512,512]{2,1,0:T(8,128)S(1)} %get-tuple-element.9.done_ref, bf16[512,1024]{1,0:T(8,128)(2,1)S(1)} %get-tuple-element.10.left_hi, bf16[512,1024]{1,0:T(8,128)(2,1)S(1)} %get-tuple-element.11.left_lo, f32[1,2,128,128]{3,2,1,0:T(8,128)S(1)} %get-tuple-element.12.last_block), custom_call_target="tpu_custom_call" | custom-call | tf_op jit(solution)/shard_map/pallas_call | solution.py:466
